TPU v7x, 32 devices: a whole 2x2x4 slice. The times are simulated.
32 devices in a mesh: groups: 2 (over y), mem: 4 (over z), head: 2 (over x), width: 2 (over core).
Axes of the slice: x: 2, y: 2, z: 4, core: 2. Of those that a mesh axis runs over, the one named last changes fastest.
Arguments:
- residual_in: bfloat16 [64, 5120], P('groups', 'mem'), parts along dimension 0, may hold values from -26 to 26
- attention_gain: float32 [5120], P('mem'), may hold values from 0.5 to 1.5
- query_weight: bfloat16 [5120, 8192], P('mem', ('head', 'width')), may hold values from -0.078125 to 0.078125
- key_weight: bfloat16 [5120, 1024], P('mem', ('head', 'width')), may hold values from -0.078125 to 0.078125
- value_weight: bfloat16 [5120, 1024], P('mem', ('head', 'width')), may hold values from -0.078125 to 0.078125
- query_norm: float32 [128], replicated, may hold values from 0.25 to 1.75
- key_norm: float32 [128], replicated, may hold values from 0.1 to 1.9
- cache_keys: bfloat16 [65536, 8, 128], P(('groups', 'mem'), ('head', 'width')), parts along dimension 0, may hold values from -480 to 480
- cache_values: bfloat16 [65536, 8, 128], P(('groups', 'mem'), ('head', 'width')), parts along dimension 0, may hold values from -12 to 12
- slot_request: int32 [65536], P(('groups', 'mem')), parts along dimension 0, may hold values from 0 to 16, as said below
- lengths: int32 [32], P('groups'), parts along dimension 0, may hold values from 1056 to 1760, as said below
- output_weight: bfloat16 [8192, 5120], P(('head', 'width'), 'mem'), may hold values from -0.0625 to 0.0625
- second_gain: float32 [5120], P('mem'), may hold values from 0.5 to 1.5
- gate_weight: bfloat16 [5120, 25600], P('mem', ('head', 'width')), may hold values from -0.078125 to 0.078125
- up_weight: bfloat16 [5120, 25600], P('mem', ('head', 'width')), may hold values from -0.078125 to 0.078125
- down_weight: bfloat16 [25600, 5120], P(('head', 'width'), 'mem'), may hold values from -0.0390625 to 0.0390625
Outputs:
- layer_out: bfloat16 [64, 5120], P('groups', 'mem'), parts along dimension 0
There are 2 independent parts, one for each index of `groups`. A program takes and returns all parts, laid end to end along the dimension named above; an argument that names none is the same for every part. Nothing has to cross between parts.
Inputs may be any that keep to these rules, and one draw needn't show every extreme that they name: slot_request[s] names the request whose cached token sits in slot s, or is 16 for an empty slot. On each owner (each aligned block of 8192 slots along mem) the used slots come first; taking owners in order and their used slots in order, requests 0 to 15 follow one another in consecutive slots, so a request may continue on the next owner, but on no further one: a request's slots lie on at most two consecutive owners. Request r has exactly lengths[r] slots. Some owner has all its slots used. lengths[r] is the number of cached tokens of request r; its new tokens stand at positions lengths[r] and lengths[r] + 1.
All inputs are finite; a program needn't handle non-finite values.
Results may differ from a plain program's by a relative error of at most 0.0095.
The roundings to bfloat16 on the way count: a program that leaves them out, or rounds other values in their place, can miss the bound.
Values may be sent and summed in bfloat16 or wider, within the bound.
A program may use at most 128 MiB of HBM per device.

v0:
```python
import math

import jax
import jax.numpy as jnp
from jax import lax
from jax.sharding import PartitionSpec as P

D = 5120


epsilon = 1e-06
rope_base = 1000000.0
floor_score = -1e30


def combined_all(value, axis, join):
    pieces = jax.tree.map(lambda part: lax.all_gather(part, axis), value)
    head = jax.tree.map(lambda part: part[0], pieces)
    tail = jax.tree.map(lambda part: part[1:], pieces)
    running, _ = lax.scan(lambda running, slab: (join(running, slab), None), head, tail)
    return running


def rotate(values, places):
    breadth = values.shape[-1]
    halfway = breadth // 2
    frequency = rope_base ** (-(jnp.arange(halfway, dtype=jnp.float32) * 2.0) / breadth)
    angles = places[..., None] * frequency
    cosine = jnp.cos(angles)
    sine_part = jnp.sin(angles)
    leading = values[..., :halfway]
    trailing = values[..., halfway:]
    return jnp.concatenate(
        [leading * cosine - trailing * sine_part, trailing * cosine + leading * sine_part], axis=-1
    )


def head_norm(values, scaling):
    mean_square = jnp.mean(values * values, axis=-1, keepdims=True)
    return values * lax.rsqrt(mean_square + epsilon) * scaling


def combine(first, second):
    first_top, first_sum, first_acc = first
    second_top, second_sum, second_acc = second
    highest = jnp.maximum(first_top, second_top)
    first_factor = jnp.exp(first_top - highest)
    second_factor = jnp.exp(second_top - highest)
    return (
        highest,
        first_sum * first_factor + second_sum * second_factor,
        first_acc * first_factor[..., None] + second_acc * second_factor[..., None],
    )


def per_device(
    residual_in,
    attention_gain,
    query_weight,
    key_weight,
    value_weight,
    query_norm,
    key_norm,
    cache_keys,
    cache_values,
    slot_request,
    lengths,
    output_weight,
    second_gain,
    gate_weight,
    up_weight,
    down_weight,
):
    row_count = residual_in.shape[0]
    requests = row_count // 2
    head_dim = query_norm.shape[0]
    kv_here = cache_keys.shape[1]
    q_here = query_weight.shape[1] // head_dim
    group_size = q_here // kv_here
    score_scale = 1.0 / math.sqrt(head_dim)
    residual = residual_in.astype(jnp.float32)
    squares = lax.psum(jnp.sum(residual * residual, axis=1), "mem")
    normed = (residual * lax.rsqrt(squares / D + epsilon)[:, None] * attention_gain).astype(
        jnp.bfloat16
    )
    query_part = jnp.dot(normed, query_weight, preferred_element_type=jnp.float32)
    key_part = jnp.dot(normed, key_weight, preferred_element_type=jnp.float32)
    value_part = jnp.dot(normed, value_weight, preferred_element_type=jnp.float32)
    offsets = jnp.arange(2, dtype=jnp.int32)
    places = (lengths[:, None] + offsets[None, :]).reshape(row_count).astype(jnp.float32)
    query_sum, key_sum, value_sum = lax.psum((query_part, key_part, value_part), "mem")
    count_rows = query_sum.shape[0]
    query_rot = rotate(
        head_norm(query_sum.reshape(count_rows, q_here, head_dim), query_norm), places[:, None]
    )
    key_rot = rotate(
        head_norm(key_sum.reshape(count_rows, kv_here, head_dim), key_norm), places[:, None]
    )
    queries = query_rot.astype(jnp.bfloat16)
    new_keys = key_rot.astype(jnp.bfloat16)
    new_values = value_sum.reshape(count_rows, kv_here, head_dim).astype(jnp.bfloat16)
    queries_split = queries.reshape(row_count, kv_here, group_size, head_dim)
    row_owner = jnp.arange(row_count, dtype=jnp.int32) // 2
    capacity = cache_keys.shape[0]
    block_size = min(1024, capacity)
    used_slots = jnp.sum((slot_request < requests).astype(jnp.int32))
    used_blocks = (used_slots + block_size - 1) // block_size
    start_state = (
        jnp.full((row_count, kv_here, group_size), floor_score, jnp.float32),
        jnp.zeros((row_count, kv_here, group_size), jnp.float32),
        jnp.zeros((row_count, kv_here, group_size, head_dim), jnp.float32),
    )

    def visit_block(counter, carried):
        highest, summed, running = carried
        first_slot = counter * block_size
        key_block = lax.dynamic_slice_in_dim(cache_keys, first_slot, block_size, 0)
        value_block = lax.dynamic_slice_in_dim(cache_values, first_slot, block_size, 0)
        owner_block = lax.dynamic_slice_in_dim(slot_request, first_slot, block_size, 0)
        scores = (
            jnp.einsum(
                "bkgd,skd->bkgs", queries_split, key_block, preferred_element_type=jnp.float32
            )
            * score_scale
        )
        matches = (owner_block[None, :] == row_owner[:, None])[:, None, None, :]
        block_top = jnp.max(jnp.where(matches, scores, floor_score), axis=-1)
        updated = jnp.maximum(highest, block_top)
        weights = jnp.where(matches, jnp.exp(scores - updated[..., None]), 0.0)
        factor = jnp.exp(highest - updated)
        summed = summed * factor + jnp.sum(weights, axis=-1)
        running = running * factor[..., None] + jnp.einsum(
            "bkgs,skd->bkgd",
            weights.astype(jnp.bfloat16),
            value_block,
            preferred_element_type=jnp.float32,
        )
        return (updated, summed, running)

    highest, summed, running = lax.fori_loop(0, used_blocks, visit_block, start_state)
    highest, summed, running = combined_all((highest, summed, running), "mem", combine)
    query_pairs = queries.reshape(requests, 2, kv_here, group_size, head_dim)
    key_pairs = new_keys.reshape(requests, 2, kv_here, head_dim)
    value_pairs = new_values.reshape(requests, 2, kv_here, head_dim)
    allowed = (offsets[None, :] <= offsets[:, None])[None, :, None, None, :]
    allowed_rows = jnp.broadcast_to(allowed, (requests, 2, kv_here, group_size, 2)).reshape(
        row_count, kv_here, group_size, 2
    )
    own_scores = (
        jnp.einsum("rtkgd,rskd->rtkgs", query_pairs, key_pairs, preferred_element_type=jnp.float32)
        * score_scale
    )
    own_scores = jnp.where(allowed, own_scores, floor_score).reshape(
        row_count, kv_here, group_size, 2
    )
    final_top = jnp.maximum(highest, jnp.max(own_scores, axis=-1))
    own_weights = jnp.where(allowed_rows, jnp.exp(own_scores - final_top[..., None]), 0.0)
    factor = jnp.exp(highest - final_top)
    summed = summed * factor + jnp.sum(own_weights, axis=-1)
    own_rounded = own_weights.astype(jnp.bfloat16).reshape(requests, 2, kv_here, group_size, 2)
    own_values = jnp.einsum(
        "rtkgs,rskd->rtkgd", own_rounded, value_pairs, preferred_element_type=jnp.float32
    )
    running = running * factor[..., None] + own_values.reshape(
        row_count, kv_here, group_size, head_dim
    )
    attended = (
        (running / summed[..., None]).reshape(row_count, q_here * head_dim).astype(jnp.bfloat16)
    )
    projected = lax.psum(
        jnp.dot(attended, output_weight, preferred_element_type=jnp.float32), ("head", "width")
    )
    middle = (residual + projected).astype(jnp.bfloat16)
    middle_wide = middle.astype(jnp.float32)
    squares_mid = lax.psum(jnp.sum(middle_wide * middle_wide, axis=1), "mem")
    normed_mid = (middle_wide * lax.rsqrt(squares_mid / D + epsilon)[:, None] * second_gain).astype(
        jnp.bfloat16
    )
    gate_part = jnp.dot(normed_mid, gate_weight, preferred_element_type=jnp.float32)
    up_part = jnp.dot(normed_mid, up_weight, preferred_element_type=jnp.float32)
    gate_sum, up_sum = (
        lax.psum_scatter(gate_part, "mem", scatter_dimension=0, tiled=True),
        lax.psum_scatter(up_part, "mem", scatter_dimension=0, tiled=True),
    )
    activated = lax.all_gather(
        (jax.nn.silu(gate_sum) * up_sum).astype(jnp.bfloat16), "mem", axis=0, tiled=True
    )
    down_sum = lax.psum(
        jnp.dot(activated, down_weight, preferred_element_type=jnp.float32), ("head", "width")
    )
    return (middle_wide + down_sum).astype(jnp.bfloat16)


def solution(mesh):
    return jax.shard_map(
        per_device,
        mesh=mesh,
        in_specs=(
            P("groups", "mem"),
            P("mem"),
            P("mem", ("head", "width")),
            P("mem", ("head", "width")),
            P("mem", ("head", "width")),
            P(),
            P(),
            P(("groups", "mem"), ("head", "width"), None),
            P(("groups", "mem"), ("head", "width"), None),
            P(("groups", "mem")),
            P("groups"),
            P(("head", "width"), "mem"),
            P("mem"),
            P("mem", ("head", "width")),
            P("mem", ("head", "width")),
            P(("head", "width"), "mem"),
        ),
        out_specs=P("groups", "mem"),
        check_vma=False,
    )
```

profile of v0, /device:TPU:0, one launch (start us, length us, event | category | flops | bytes accessed | tf_op | source)
XLA Modules:
  0.0 317.9 jit_solution(10210930667824503828)
XLA Ops:
  7.7 13.5 %psum.49 = f32[32]{0:T(128)S(1)} all-reduce(f32[32]{0:T(128)S(1)} %fusion.24), channel_id=1, replica_groups=mesh['groups'=2,'mem'=4,'head'=2,'width'=2] {'mem'}, use_global_device_ids=true, to_apply=%region_2.0 | all-reduce | flops 32 | bytes 256 | tf_op jit(solution)/shard_map/psum | solution.py:82
  21.1 3.6 %convolution_bitcast_fusion.1 = f32[4,8,16,128]{3,1,2,0:T(8,128)S(1)} fusion(bf16[1280,2048]{1,0:T(8,128)(2,1)} %param.22, bf16[32,1280]{1,0:T(8,128)(2,1)} %param.20, f32[1280]{0:T(1024)} %param.21, f32[32]{0:T(128)S(1)} %add_rsqrt_fusion.3), kind=kOutput, calls=%fused_computation.38 | convolution fusion | flops 167936000 | bytes 5592192 | tf_op jit(solution)/shard_map/dot_general | solution.py:86
  27.3 32.1 %all-reduce.5.cloned.1.call-done = f32[32,16,128]{2,1,0:T(8,128)} async-done(((f32[32,16,128]{2,1,0:T(8,128)}), f32[32,16,128]{2,1,0:T(8,128)}) %all-reduce.5.cloned.1.call-update) | async-done | bytes 262160 | tf_op jit(solution)/shard_map/psum | solution.py:91
  62.2 31.8 %while.30 = (s32[]{:T(128)}, f32[32,2,8]{0,2,1:T(8,128)S(1)}, f32[32,2,8]{0,2,1:T(8,128)S(1)}, f32[32,2,8,128]{3,0,2,1:T(8,128)S(1)}, s32[]{:T(128)}, /*index=5*...) while((s32[]{:T(128)}, f32[32,2,8]{0,2,1:T(8,128)S(1)}, ...), condition=%wide.region_8.9_spmd.clone, body=%wide.region_5.8_spmd.clone.sunk | while | flops 274367744 | bytes 10269107 | solution.py:140
  62.3 2.0 constant_dynamic-slice_fusion.6
  66.3 1.9 constant_dynamic-slice_fusion.6
  70.3 1.9 constant_dynamic-slice_fusion.6
  74.3 1.9 constant_dynamic-slice_fusion.6
  78.2 1.9 constant_dynamic-slice_fusion.6
  82.2 1.9 constant_dynamic-slice_fusion.6
  86.2 1.9 constant_dynamic-slice_fusion.6
  95.3 20.1 %all-reduce = (bf16[32,256]{1,0:T(8,128)(2,1)S(1)}, f32[32,2,128]{2,0,1:T(8,128)S(1)}) all-reduce(f32[32,256]{1,0:T(8,128)S(1)} %fusion.45, f32[32,2,128]{2,0,1:T(8,128)S(1)} %bitcast.129), channel_id=1, replica_groups=mesh['groups'=2,'mem'=4,'head'=2,'width'=2] {'mem'}, use_global_device_ids=true, to_apply=%region_14.15 | all-reduce | flops 16384 | bytes 114688 | tf_op jit(solution)/shard_map/psum | solution.py:91
  115.8 14.2 %all-gather.1 = f32[128,2,8]{2,1,0:T(2,128)S(1)} all-gather(f32[32,2,8]{2,1,0:T(2,128)S(1)} %copy.92), channel_id=3, replica_groups=mesh['groups'=2,'mem'=4,'head'=2,'width'=2] {'mem'}, dimensions={0}, use_global_device_ids=true | all-gather | bytes 10240 | tf_op jit(solution)/shard_map/all_gather | solution.py:17
  130.0 13.3 %all-gather = f32[128,2,8]{2,1,0:T(2,128)S(1)} all-gather(f32[32,2,8]{2,1,0:T(2,128)S(1)} %copy.91), channel_id=2, replica_groups=mesh['groups'=2,'mem'=4,'head'=2,'width'=2] {'mem'}, dimensions={0}, use_global_device_ids=true | all-gather | bytes 10240 | tf_op jit(solution)/shard_map/all_gather | solution.py:17
  149.7 4.1 %fusion.32 = f32[32,1280]{1,0:T(8,128)} fusion(bf16[2048,1280]{1,0:T(8,128)(2,1)} %param.31, bf16[4,8,16,128]{3,2,1,0:T(8,128)(2,1)S(1)} %bitcast.122), kind=kOutput, calls=%fused_computation.66 | convolution fusion | flops 167772160 | bytes 5537792 | tf_op jit(solution)/shard_map/dot_general | solution.py:171
  153.9 30.1 %all-reduce.7.cloned.1.call-done = f32[32,1280]{1,0:T(8,128)} async-done(((f32[32,1280]{1,0:T(8,128)}), f32[32,1280]{1,0:T(8,128)}) %all-reduce.7.cloned.1.call-update) | async-done | bytes 163856 | tf_op jit(solution)/shard_map/psum | solution.py:170
  185.1 11.7 %psum.54 = f32[32]{0:T(128)S(1)} all-reduce(f32[32]{0:T(128)S(1)} %get-tuple-element.230), channel_id=1, replica_groups=mesh['groups'=2,'mem'=4,'head'=2,'width'=2] {'mem'}, use_global_device_ids=true, to_apply=%region_18.19 | all-reduce | flops 32 | bytes 256 | tf_op jit(solution)/shard_map/psum | solution.py:175
  196.8 9.6 %fusion.37 = f32[32,6400]{1,0:T(8,128)} fusion(bf16[1280,6400]{1,0:T(8,128)(2,1)} %param.34, bf16[32,1280]{1,0:T(8,128)(2,1)S(1)} %get-tuple-element.231, f32[1280]{0:T(1024)S(1)} %copy-done.5, f32[32]{0:T(128)S(1)} %add_rsqrt_fusion.2), kind=kOutput, calls=%fused_computation.82 | convolution fusion | flops 524451840 | bytes 17290368 | tf_op jit(solution)/shard_map/dot_general | solution.py:180
  206.6 9.7 %fusion.39 = f32[32,6400]{1,0:T(8,128)} fusion(bf16[1280,6400]{1,0:T(8,128)(2,1)} %param.33, bf16[32,1280]{1,0:T(8,128)(2,1)S(1)} %get-tuple-element.231, f32[1280]{0:T(1024)S(1)} %copy-done.5, f32[32]{0:T(128)S(1)} %add_rsqrt_fusion.2), kind=kOutput, calls=%fused_computation.83 | convolution fusion | flops 524451840 | bytes 17290368 | tf_op jit(solution)/shard_map/dot_general | solution.py:179
  216.4 11.0 %reduce-scatter.5.cloned.1.call-done = f32[8,6400]{1,0:T(8,128)} async-done(((f32[32,6400]{1,0:T(8,128)}), f32[8,6400]{1,0:T(8,128)}) %reduce-scatter.5.cloned.1.call-update) | async-done | bytes 204816 | tf_op jit(solution)/shard_map/reduce_scatter | solution.py:183
  227.4 25.2 %reduce-scatter.3.cloned.1.call-done = f32[8,6400]{1,0:T(8,128)} async-done(((f32[32,6400]{1,0:T(8,128)}), f32[8,6400]{1,0:T(8,128)}) %reduce-scatter.3.cloned.1.call-update) | async-done | bytes 204816 | tf_op jit(solution)/shard_map/reduce_scatter | solution.py:182
  253.7 15.2 %all_gather.27 = bf16[32,6400]{1,0:T(8,128)(2,1)S(1)} all-gather(bf16[8,6400]{1,0:T(8,128)(2,1)S(1)} %multiply_convert_fusion), channel_id=1, replica_groups=mesh['groups'=2,'mem'=4,'head'=2,'width'=2] {'mem'}, dimensions={0}, use_global_device_ids=true | all-gather | bytes 512000 | tf_op jit(solution)/shard_map/all_gather | solution.py:185
  268.9 9.3 %fusion.52 = f32[32,1280]{1,0:T(8,128)} fusion(bf16[32,6400]{1,0:T(8,128)(2,1)S(1)} %all_gather.27, bf16[6400,1280]{1,0:T(8,128)(2,1)} %param.35), kind=kOutput, calls=%fused_computation.100 | convolution fusion | flops 524288000 | bytes 16957440 | tf_op jit(solution)/shard_map/dot_general | solution.py:189
  278.2 31.2 %all-reduce.9.cloned.1.call-done = f32[32,1280]{1,0:T(8,128)} async-done(((f32[32,1280]{1,0:T(8,128)}), f32[32,1280]{1,0:T(8,128)}) %all-reduce.9.cloned.1.call-update) | async-done | bytes 163856 | tf_op jit(solution)/shard_map/psum | solution.py:188
  (182 shorter events, 36.8 us)
Async XLA Ops:
  6.5 88.2 %copy-start = (bf16[1280,256]{1,0:T(8,128)(2,1)S(1)}, bf16[1280,256]{1,0:T(8,128)(2,1)}, u32[]{:S(2)}) copy-start(bf16[1280,256]{1,0:T(8,128)(2,1)} %param.23) | copy-start | bytes 1966084
  6.5 19.0 %copy-start.6 = (s32[8192]{0:T(1024)S(1)}, s32[8192]{0:T(1024)}, u32[]{:S(2)}) copy-start(s32[8192]{0:T(1024)} %param.29) | copy-start | bytes 98308
  6.5 19.8 %copy-start.10 = (s32[16]{0:T(128)S(1)}, s32[16]{0:T(128)}, u32[]{:S(2)}) copy-start(s32[16]{0:T(128)} %param.30) | copy-start | bytes 196
  6.5 54.0 %copy-start.8 = (f32[128]{0:T(128)S(1)}, f32[128]{0:T(128)}, u32[]{:S(2)}) copy-start(f32[128]{0:T(128)} %param.25) | copy-start | bytes 1540
  6.5 52.9 %all-reduce.5.cloned.1.call-start = ((), (), s32[]{:S(2)}) async-start(), calls=%async_computation.2 | async-start | bytes 524288 | tf_op jit(solution)/shard_map/psum | solution.py:91
  25.5 119.1 %all-gather.5.cloned.1.call-start = ((), (), s32[]{:S(2)}) async-start(), calls=%async_computation.7 | async-start | bytes 1310720 | tf_op jit(solution)/shard_map/all_gather | solution.py:17
  62.1 32.7 %copy-start.2 = (bf16[32,1280]{1,0:T(8,128)(2,1)S(1)}, bf16[32,1280]{1,0:T(8,128)(2,1)}, u32[]{:S(2)}) copy-start(bf16[32,1280]{1,0:T(8,128)(2,1)} %param.20) | copy-start | bytes 245764
  62.1 32.7 %copy-start.7 = (f32[1280]{0:T(1024)S(1)}, f32[1280]{0:T(1024)}, u32[]{:S(2)}) copy-start(f32[1280]{0:T(1024)} %param.21) | copy-start | bytes 15364
  62.1 32.9 %copy-start.4 = (bf16[1280,256]{1,0:T(8,128)(2,1)S(1)}, bf16[1280,256]{1,0:T(8,128)(2,1)}, u32[]{:S(2)}) copy-start(bf16[1280,256]{1,0:T(8,128)(2,1)} %param.24) | copy-start | bytes 1966084
  62.2 53.3 %copy-start.9 = (f32[128]{0:T(128)S(1)}, f32[128]{0:T(128)}, u32[]{:S(2)}) copy-start(f32[128]{0:T(128)} %param.26) | copy-start | bytes 1540
  94.0 0.7 copy-start.3
  94.7 89.3 %all-reduce.7.cloned.1.call-start = ((), (), s32[]{:S(2)}) async-start(), calls=%async_computation.3 | async-start | bytes 327680 | tf_op jit(solution)/shard_map/psum | solution.py:170
  148.6 48.2 %copy-start.5 = (f32[1280]{0:T(1024)S(1)}, f32[1280]{0:T(1024)}, u32[]{:S(2)}) copy-start(f32[1280]{0:T(1024)} %param.32) | copy-start | bytes 15364
  153.9 73.5 %reduce-scatter.5.cloned.1.call-start = ((), (), s32[]{:S(2)}) async-start(), calls=%async_computation.5 | async-start | bytes 1024000 | tf_op jit(solution)/shard_map/reduce_scatter | solution.py:183
  206.4 46.3 %reduce-scatter.3.cloned.1.call-start = ((), (), s32[]{:S(2)}) async-start(), calls=%async_computation.4 | async-start | bytes 1024000 | tf_op jit(solution)/shard_map/reduce_scatter | solution.py:182
  216.3 93.1 %all-reduce.9.cloned.1.call-start = ((), (), s32[]{:S(2)}) async-start(), calls=%async_computation.6 | async-start | bytes 327680 | tf_op jit(solution)/shard_map/psum | solution.py:188
  268.9 42.1 %copy-start.1 = (bf16[1280,256]{1,0:T(8,128)(2,1)S(1)}, bf16[1280,256]{1,0:T(8,128)(2,1)}, u32[]{:S(2)}) copy-start(bf16[1280,256]{1,0:T(8,128)(2,1)} %param.23) | copy-start | bytes 1966084
Sparse Core Ops, SparseCore 0:
  25.6 33.7 all-reduce.4
  94.8 30.4 all-gather.4
  154.0 29.9 all-reduce.6
  206.5 20.8 reduce-scatter.4
  229.6 22.9 reduce-scatter.2
  278.3 31.0 all-reduce.8
where the time goes:
time: 319 us; the launch traced here: 318 us
  waiting for transfers between devices  130 us (41%)
  blocking collectives  87.9 us (28%)
  matrix products  47.6 us (15%)
  local copies, waits for them, and re-layouts  21.2 us (7%)
  other arithmetic  15.7 us (5%)
  between operations  14.6 us (5%)
    psum x1, waiting for transfers between devices, per_device(): lax.psum((query_part, key_part, value_part), 'mem')  32.1 us
    psum x1, waiting for transfers between devices, per_device(): lax.psum(jnp.dot(activated, down_weight, preferred_element_type=jnp.float...  31.2 us
    psum x1, waiting for transfers between devices, per_device(): lax.psum(jnp.dot(attended, output_weight, preferred_element_type=jnp.floa...  30.1 us
    all_gather x2, blocking collectives, combined_all(): pieces = jax.tree.map(lambda part: lax.all_gather(part, axis), value)  27.5 us
    reduce_scatter x1, waiting for transfers between devices, per_device(): lax.psum_scatter(gate_part, 'mem', scatter_dimension=0, tiled=True)  25.2 us
    psum x1, blocking collectives, per_device(): lax.psum((query_part, key_part, value_part), 'mem')  20.1 us
    dynamic_slice x8, local copies, waits for them, and re-layouts, visit_block(): lax.dynamic_slice_in_dim(cache_values, first_slot, block_size, 0)  15.5 us
    all_gather x1, blocking collectives, per_device(): lax.all_gather((jax.nn.silu(gate_sum) * up_sum).astype(jnp.bfloat16), 'me...  15.2 us
  transfers between devices with their start and end apart: 6, of which 5 were waited for; matrix products, arithmetic and copies ran while one was open for 4% of the time, Pallas kernels for 0%

commit v1 on v0

v1 whole, which is shorter than its diff:
```python
import functools
import math

import jax
import jax.numpy as jnp
from jax import lax
from jax.experimental import pallas as pl
from jax.experimental.pallas import tpu as pltpu
from jax.sharding import PartitionSpec as P

epsilon = 1e-06
rope_base = 1000000.0
floor_score = -1e30
LANES = 128
CHUNK = 1792
VMEM_LIMIT = 67043328
f32 = jnp.float32
bf16 = jnp.bfloat16


def tile_of(size, most):
    best = LANES
    for t in range(LANES, most + 1, LANES):
        if size % t == 0:
            best = t
    return best


class Ring:
    def __init__(self, axes, sizes):
        self.axes, self.sizes = axes, sizes
        self.n = math.prod(sizes)
        self.me = 0
        for axis, size in zip(axes, sizes):
            self.me = self.me * size + lax.axis_index(axis)

    def peer(self, d):
        return lax.rem(self.me + d, self.n)

    def ident(self, p):
        if len(self.axes) == 1:
            return {self.axes[0]: p}
        return {self.axes[0]: p // self.sizes[1], self.axes[1]: p % self.sizes[1]}

    def order(self):
        half = self.n // 2
        return sorted(range(1, self.n), key=lambda d: abs(d - half))

    def greet(self, barrier):
        for d in range(1, self.n):
            pl.semaphore_signal(
                barrier, inc=1, device_id=self.ident(self.peer(d)),
                device_id_type=pl.DeviceIdType.MESH,
            )

    def copies(self, src, dst, send, recv):
        out = []
        for d in self.order():
            p = self.peer(d)
            out.append(
                pltpu.make_async_remote_copy(
                    src_ref=src(p), dst_ref=dst(d), send_sem=send(d - 1), recv_sem=recv(d - 1),
                    device_id=self.ident(p), device_id_type=pl.DeviceIdType.MESH,
                )
            )
        return out


def start_all(copies):
    for c in copies:
        c.start()


def recv_all(copies):
    for c in copies:
        c.wait_recv()


def send_all(copies):
    for c in copies:
        c.wait_send()


def qkv_kernel(
    n, q_here, kv_here, res_ref, gain_ref, qn_ref, kn_ref, cos_ref, sin_ref, wq, wk, wv, out_ref,
    w, sq, sqr, part, partr, gath, wsem, s0, r0, s1, r1, s2, r2,
):
    ring = Ring(("mem",), (n,))
    rows, dl = res_ref.shape
    rn, cols = part.shape[1], part.shape[2]
    cq, ck = wq.shape[1], wk.shape[1]
    loads = [
        pltpu.make_async_copy(wq, w.at[:, pl.ds(0, cq)], wsem.at[0]),
        pltpu.make_async_copy(wk, w.at[:, pl.ds(cq, ck)], wsem.at[1]),
        pltpu.make_async_copy(wv, w.at[:, pl.ds(cq + ck, ck)], wsem.at[2]),
    ]
    start_all(loads)
    res = res_ref[...].astype(f32)
    sums = jnp.sum(res * res, axis=1, keepdims=True)
    sq[...] = jnp.broadcast_to(sums, sq.shape)
    barrier = pltpu.get_barrier_semaphore()
    ring.greet(barrier)
    pl.semaphore_wait(barrier, n - 1)
    c0 = ring.copies(lambda p: sq, lambda d: sqr.at[d - 1], lambda i: s0.at[i], lambda i: r0.at[i])
    start_all(c0)
    recv_all(c0)
    total = sq[...]
    for d in range(n - 1):
        total = total + sqr[d]
    scale = lax.rsqrt(total / (dl * n) + epsilon)[:, :1]
    normed = (res * scale * gain_ref[...]).astype(bf16)
    for c in loads:
        c.wait()
    tn = tile_of(cols, 640)
    for t in range(cols // tn):
        block = jnp.dot(normed, w[:, t * tn : (t + 1) * tn], preferred_element_type=f32)
        part[:, :, t * tn : (t + 1) * tn] = block.reshape(n, rn, tn)
    c1 = ring.copies(
        lambda p: part.at[p], lambda d: partr.at[d - 1], lambda i: s1.at[i], lambda i: r1.at[i]
    )
    start_all(c1)
    recv_all(c1)
    here = pl.ds(ring.me * rn, rn)
    cosine, sine = cos_ref[here, :], sin_ref[here, :]
    for h in range(q_here + 2 * kv_here):
        span = slice(h * LANES, (h + 1) * LANES)
        x = part[ring.me, :, span]
        for d in range(n - 1):
            x = x + partr[d, :, span]
        if h < q_here + kv_here:
            gain = qn_ref[...] if h < q_here else kn_ref[...]
            square = jnp.mean(x * x, axis=-1, keepdims=True)
            x = x * lax.rsqrt(square + epsilon) * gain
            x = x * cosine + pltpu.roll(x, LANES // 2, 1) * sine
        gath[ring.me, :, span] = x.astype(bf16)
    c2 = ring.copies(
        lambda p: gath.at[ring.me], lambda d: gath.at[ring.me],
        lambda i: s2.at[i], lambda i: r2.at[i],
    )
    start_all(c2)
    recv_all(c2)
    out_ref[...] = gath[...]
    send_all(c0 + c1 + c2)


def attend_kernel(
    n, kv, starts, ends, q_ref, nk_ref, nv_ref, k_ref, v_ref, o_ref, st_ref, lse,
):
    requests, m_rows, hd = q_ref.shape
    q_here = m_rows // 2
    group = q_here // kv
    cap = k_ref.shape[0] // kv
    chunk = min(CHUNK, cap)
    rpc = requests // n
    me = lax.axis_index("mem")
    score_scale = 1.0 / math.sqrt(hd)
    row = lax.broadcasted_iota(jnp.int32, (m_rows, chunk * kv), 0)
    col = lax.broadcasted_iota(jnp.int32, (m_rows, chunk * kv), 1)
    same = ((row // group) % kv) == (col % kv)

    def visit(r, unused):
        s, e = starts[r], ends[r]
        q = q_ref[r]
        qf = q.astype(f32)
        mine = (r // rpc) == me
        keys, vals = nk_ref[r], nv_ref[r]
        tops, sums, accs = [], [], []
        for t in range(2):
            for k in range(kv):
                b = (t * kv + k) * group
                qb = qf[b : b + group]
                sc = [
                    jnp.sum(qb * keys[u * kv + k : u * kv + k + 1], axis=-1, keepdims=True)
                    * score_scale
                    for u in range(t + 1)
                ]
                top = sc[0] if t == 0 else jnp.maximum(sc[0], sc[1])
                ws = [jnp.exp(x - top) for x in sc]
                total, acc = 0.0, 0.0
                for u, x in enumerate(ws):
                    total = total + x
                    acc = acc + x.astype(bf16).astype(f32) * vals[u * kv + k : u * kv + k + 1]
                tops.append(top)
                sums.append(total)
                accs.append(acc)
        top = jnp.where(mine, jnp.concatenate(tops, axis=0), floor_score)
        total = jnp.where(mine, jnp.concatenate(sums, axis=0), 0.0)
        acc = jnp.where(mine, jnp.concatenate(accs, axis=0), 0.0)
        base = (s // 16) * 16
        trips = jnp.where(e > s, (e - base + chunk - 1) // chunk, 0)

        def step(c, carried):
            top, total, acc = carried
            want = base + c * chunk
            at = jnp.minimum(want, cap - chunk)
            low = jnp.maximum(s, want)
            span = pl.ds(pl.multiple_of(at * kv, 16), chunk * kv)
            scores = (
                lax.dot_general(
                    q, k_ref[span, :], (((1,), (1,)), ((), ())), preferred_element_type=f32
                )
                * score_scale
            )
            valid = same & (col >= (low - at) * kv) & (col < (e - at) * kv)
            scores = jnp.where(valid, scores, floor_score)
            new = jnp.maximum(top, jnp.max(scores, axis=-1, keepdims=True))
            weights = jnp.exp(scores - new)
            factor = jnp.exp(top - new)
            total = total * factor + jnp.sum(weights, axis=-1, keepdims=True)
            acc = acc * factor + jnp.dot(
                weights.astype(bf16), v_ref[span, :], preferred_element_type=f32
            )
            return new, total, acc

        top, total, acc = lax.fori_loop(0, trips, step, (top, total, acc))
        some = total > 0.0
        safe = jnp.where(some, total, 1.0)
        o_ref[r] = acc / safe
        lse[r] = jnp.broadcast_to(jnp.where(some, top + jnp.log(safe), floor_score), (m_rows, LANES))
        return unused

    lax.fori_loop(0, requests, visit, 0)
    for j in range(n):
        flat = lse[j * rpc : (j + 1) * rpc].reshape(rpc * m_rows, LANES)
        st_ref[j] = flat.T[:8]


def tail_kernel(
    n, hwn, q_here, o_ref, st_ref, res_ref, gain_ref, wo_h, wg_h, wu_h, wd_h, out_ref,
    wo, wg, wu, wd, osend, orecv, strecv, flat, att, opart, orow, midn, sq, sqr,
    gsend, grecv, gown, act, dpart, drecv, fin,
    wosem, wgsem, wusem, wdsem,
    sa, ra, sb, rb, sc, rc, sd, rd, se, re, sf, rf, sg, rg, sh, rh, si, ri, sj, rj,
):
    mem = Ring(("mem",), (n,))
    hw = Ring(("head", "width"), hwn)
    nh = hw.n
    tiles, dl, tn = wg.shape
    rn = att.shape[1]
    rh_rows = midn.shape[1]
    per = flat.shape[0]
    load_o = pltpu.make_async_copy(wo_h, wo, wosem)
    load_o.start()

    def gate_load(t):
        span = pl.ds(pl.multiple_of(t * tn, LANES), tn)
        return (
            pltpu.make_async_copy(wg_h.at[:, span], wg.at[t], wgsem.at[t]),
            pltpu.make_async_copy(wu_h.at[:, span], wu.at[t], wusem.at[t]),
        )

    def down_load(t):
        span = pl.ds(pl.multiple_of(t * tn, LANES), tn)
        return pltpu.make_async_copy(wd_h.at[span, :], wd.at[t], wdsem.at[t])

    @pl.loop(0, tiles)
    def _(t):
        start_all(gate_load(t))

    @pl.loop(0, tiles)
    def _(t):
        down_load(t).start()

    osend[...] = o_ref[...].astype(bf16)
    barrier = pltpu.get_barrier_semaphore()
    mem.greet(barrier)
    hw.greet(barrier)
    pl.semaphore_wait(barrier, n - 1 + nh - 1)

    ca = mem.copies(
        lambda p: st_ref.at[p], lambda d: strecv.at[d - 1], lambda i: sa.at[i], lambda i: ra.at[i]
    )
    cb = mem.copies(
        lambda p: osend.at[p], lambda d: orecv.at[d - 1], lambda i: sb.at[i], lambda i: rb.at[i]
    )
    start_all(ca)
    start_all(cb)
    recv_all(ca)

    def spread(x):
        return jnp.broadcast_to(x[0:1], (LANES, per)).T

    stats = [spread(st_ref[mem.me])] + [spread(strecv[d]) for d in range(n - 1)]
    top = functools.reduce(jnp.maximum, stats)
    weights = [jnp.exp(x - top) for x in stats]
    total = functools.reduce(lambda a, b: a + b, weights)
    recv_all(cb)
    acc = o_ref[mem.me] * weights[0]
    for d in range(n - 1):
        acc = acc + orecv[d].astype(f32) * weights[d + 1]
    flat[...] = acc / total
    for h in range(q_here):
        att[mem.me, :, h * LANES : (h + 1) * LANES] = flat[pl.ds(h, rn, stride=q_here), :].astype(
            bf16
        )
    cc = mem.copies(
        lambda p: att.at[mem.me], lambda d: att.at[mem.me], lambda i: sc.at[i], lambda i: rc.at[i]
    )
    start_all(cc)
    load_o.wait()
    recv_all(cc)
    rows = n * rn
    attended = att[...].astype(f32).reshape(rows, att.shape[2]).astype(bf16)

    to = dl if dl % LANES else tile_of(dl, 640)
    for t in range(dl // to):
        block = jnp.dot(attended, wo[:, t * to : (t + 1) * to], preferred_element_type=f32)
        opart[:, :, t * to : (t + 1) * to] = block.reshape(nh, rh_rows, to)
    cd = hw.copies(
        lambda p: opart.at[p], lambda d: orow.at[d - 1], lambda i: sd.at[i], lambda i: rd.at[i]
    )
    start_all(cd)
    recv_all(cd)
    mid = opart[hw.me]
    for d in range(nh - 1):
        mid = mid + orow[d]
    mid = (res_ref[hw.me].astype(f32) + mid).astype(bf16).astype(f32)
    sq[...] = jnp.broadcast_to(jnp.sum(mid * mid, axis=1, keepdims=True), sq.shape)
    ce = mem.copies(lambda p: sq, lambda d: sqr.at[d - 1], lambda i: se.at[i], lambda i: re.at[i])
    start_all(ce)
    recv_all(ce)
    total = sq[...]
    for d in range(n - 1):
        total = total + sqr[d]
    scale = lax.rsqrt(total / (dl * n) + epsilon)[:, :1]
    midn[hw.me] = (mid * scale * gain_ref[...]).astype(bf16)
    cf = hw.copies(
        lambda p: midn.at[hw.me], lambda d: midn.at[hw.me], lambda i: sf.at[i], lambda i: rf.at[i]
    )
    start_all(cf)
    recv_all(cf)
    normed = midn[...].astype(f32).reshape(rows, dl).astype(bf16)

    def cg(t):
        return mem.copies(
            lambda p: gsend.at[t, p], lambda d: grecv.at[t, d - 1],
            lambda i: sg.at[t, i], lambda i: rg.at[t, i],
        )

    def ch(t):
        return mem.copies(
            lambda p: act.at[t, mem.me], lambda d: act.at[t, mem.me],
            lambda i: sh.at[t, i], lambda i: rh.at[t, i],
        )

    @pl.loop(0, tiles)
    def _(t):
        for c in gate_load(t):
            c.wait()
        gate = jnp.dot(normed, wg[t], preferred_element_type=f32).reshape(n, rn, tn)
        up = jnp.dot(normed, wu[t], preferred_element_type=f32).reshape(n, rn, tn)
        gown[t, :, 0] = gate
        gown[t, :, 1] = up
        gsend[t, :, 0] = gate.astype(bf16)
        gsend[t, :, 1] = up.astype(bf16)
        start_all(cg(t))

    @pl.loop(0, tiles)
    def _(t):
        recv_all(cg(t))
        both = gown[t, mem.me]
        for d in range(n - 1):
            both = both + grecv[t, d].astype(f32)
        gate, up = both[0], both[1]
        act[t, mem.me] = (gate / (1.0 + jnp.exp(-gate)) * up).astype(bf16)
        start_all(ch(t))

    dpart[...] = jnp.zeros_like(dpart)

    @pl.loop(0, tiles)
    def _(t):
        recv_all(ch(t))
        down_load(t).wait()
        block = act[t].astype(f32).reshape(rows, tn).astype(bf16)
        dpart[...] += jnp.dot(block, wd[t], preferred_element_type=f32).reshape(dpart.shape)

    ci = hw.copies(
        lambda p: dpart.at[p], lambda d: drecv.at[d - 1], lambda i: si.at[i], lambda i: ri.at[i]
    )
    start_all(ci)
    recv_all(ci)
    last = dpart[hw.me]
    for d in range(nh - 1):
        last = last + drecv[d]
    fin[hw.me] = (mid + last).astype(bf16)
    cj = hw.copies(
        lambda p: fin.at[hw.me], lambda d: fin.at[hw.me], lambda i: sj.at[i], lambda i: rj.at[i]
    )
    start_all(cj)
    recv_all(cj)
    out_ref[...] = fin[...]
    send_all(ca + cb + cc + cd + ce + cf + ci + cj)

    @pl.loop(0, tiles)
    def _(t):
        send_all(cg(t))
        send_all(ch(t))


def per_device(
    n, hwn,
    residual_in, attention_gain, query_weight, key_weight, value_weight, query_norm, key_norm,
    cache_keys, cache_values, slot_request, lengths, output_weight, second_gain, gate_weight,
    up_weight, down_weight,
):
    rows, dl = residual_in.shape
    requests = rows // 2
    hd = query_norm.shape[0]
    cap, kv, _ = cache_keys.shape
    q_here = query_weight.shape[1] // hd
    nh = math.prod(hwn)
    rn, rh = rows // n, rows // nh
    cq, ck = query_weight.shape[1], key_weight.shape[1]
    cols = cq + 2 * ck
    VM = pl.BlockSpec(memory_space=pltpu.VMEM)
    SM = pl.BlockSpec(memory_space=pltpu.SMEM)
    ANY = pl.BlockSpec(memory_space=pl.ANY)
    DMA = pltpu.SemaphoreType.DMA

    offsets = jnp.arange(2, dtype=jnp.int32)
    places = (lengths[:, None] + offsets[None, :]).reshape(rows).astype(f32)
    half = hd // 2
    frequency = rope_base ** (-(jnp.arange(half, dtype=f32) * 2.0) / hd)
    angles = places[:, None] * frequency
    cosine, sine = jnp.cos(angles), jnp.sin(angles)
    cos2 = jnp.concatenate([cosine, cosine], axis=1)
    sin2 = jnp.concatenate([-sine, sine], axis=1)
    ids = jnp.arange(requests, dtype=jnp.int32)
    starts = jnp.sum((slot_request[None, :] < ids[:, None]).astype(jnp.int32), axis=1)
    ends = jnp.sum((slot_request[None, :] <= ids[:, None]).astype(jnp.int32), axis=1)

    qkv = pl.pallas_call(
        functools.partial(qkv_kernel, n, q_here, kv),
        out_shape=jax.ShapeDtypeStruct((n, rn, cols), bf16),
        in_specs=[VM] * 6 + [ANY] * 3,
        out_specs=VM,
        scratch_shapes=[
            pltpu.VMEM((dl, cols), bf16),
            pltpu.VMEM((rows, LANES), f32),
            pltpu.VMEM((n - 1, rows, LANES), f32),
            pltpu.VMEM((n, rn, cols), f32),
            pltpu.VMEM((n - 1, rn, cols), f32),
            pltpu.VMEM((n, rn, cols), bf16),
            DMA((3,)),
        ]
        + [DMA((n - 1,))] * 6,
        compiler_params=pltpu.CompilerParams(
            collective_id=0, has_side_effects=True, vmem_limit_bytes=VMEM_LIMIT
        ),
        name="qkv",
    )(
        residual_in, attention_gain[None, :], query_norm[None, :], key_norm[None, :], cos2, sin2,
        query_weight, key_weight, value_weight,
    )
    flat = qkv.reshape(rows, cols)
    m_rows = 2 * q_here
    queries = flat[:, :cq].reshape(requests, m_rows, hd)
    new_keys = flat[:, cq : cq + ck].reshape(requests, 2 * kv, hd).astype(f32)
    new_values = flat[:, cq + ck :].reshape(requests, 2 * kv, hd).astype(f32)

    rpc = requests // n
    per = rpc * m_rows
    partial, stats = pl.pallas_call(
        functools.partial(attend_kernel, n, kv),
        out_shape=(
            jax.ShapeDtypeStruct((requests, m_rows, hd), f32),
            jax.ShapeDtypeStruct((n, 8, per), f32),
        ),
        in_specs=[SM, SM] + [VM] * 5,
        out_specs=(VM, VM),
        scratch_shapes=[pltpu.VMEM((requests, m_rows, LANES), f32)],
        compiler_params=pltpu.CompilerParams(vmem_limit_bytes=VMEM_LIMIT),
        name="attend",
    )(
        starts, ends, queries, new_keys, new_values,
        cache_keys.reshape(cap * kv, hd), cache_values.reshape(cap * kv, hd),
    )

    ffl = gate_weight.shape[1]
    tn = tile_of(ffl, 640)
    tiles = ffl // tn
    mems, hws = DMA((n - 1,)), DMA((nh - 1,))
    tms = DMA((tiles, n - 1))
    out = pl.pallas_call(
        functools.partial(tail_kernel, n, hwn, q_here),
        out_shape=jax.ShapeDtypeStruct((nh, rh, dl), bf16),
        in_specs=[VM] * 4 + [ANY] * 4,
        out_specs=VM,
        scratch_shapes=[
            pltpu.VMEM((cq, dl), bf16),
            pltpu.VMEM((tiles, dl, tn), bf16),
            pltpu.VMEM((tiles, dl, tn), bf16),
            pltpu.VMEM((tiles, tn, dl), bf16),
            pltpu.VMEM((n, per, hd), bf16),
            pltpu.VMEM((n - 1, per, hd), bf16),
            pltpu.VMEM((n - 1, 8, per), f32),
            pltpu.VMEM((per, hd), f32),
            pltpu.VMEM((n, rn, cq), bf16),
            pltpu.VMEM((nh, rh, dl), f32),
            pltpu.VMEM((nh - 1, rh, dl), f32),
            pltpu.VMEM((nh, rh, dl), bf16),
            pltpu.VMEM((rh, LANES), f32),
            pltpu.VMEM((n - 1, rh, LANES), f32),
            pltpu.VMEM((tiles, n, 2, rn, tn), bf16),
            pltpu.VMEM((tiles, n - 1, 2, rn, tn), bf16),
            pltpu.VMEM((tiles, n, 2, rn, tn), f32),
            pltpu.VMEM((tiles, n, rn, tn), bf16),
            pltpu.VMEM((nh, rh, dl), f32),
            pltpu.VMEM((nh - 1, rh, dl), f32),
            pltpu.VMEM((nh, rh, dl), bf16),
            DMA, DMA((tiles,)), DMA((tiles,)), DMA((tiles,)),
            mems, mems, mems, mems, mems, mems, hws, hws, mems, mems, hws, hws,
            tms, tms, tms, tms, hws, hws, hws, hws,
        ],
        compiler_params=pltpu.CompilerParams(
            collective_id=1, has_side_effects=True, vmem_limit_bytes=VMEM_LIMIT
        ),
        name="tail",
    )(
        partial.reshape(n, per, hd), stats, residual_in.reshape(nh, rh, dl), second_gain[None, :],
        output_weight, gate_weight, up_weight, down_weight,
    )
    return out.reshape(rows, dl)


def solution(mesh):
    hwn = (mesh.shape["head"], mesh.shape["width"])
    return jax.shard_map(
        functools.partial(per_device, mesh.shape["mem"], hwn),
        mesh=mesh,
        in_specs=(
            P("groups", "mem"),
            P("mem"),
            P("mem", ("head", "width")),
            P("mem", ("head", "width")),
            P("mem", ("head", "width")),
            P(),
            P(),
            P(("groups", "mem"), ("head", "width"), None),
            P(("groups", "mem"), ("head", "width"), None),
            P(("groups", "mem")),
            P("groups"),
            P(("head", "width"), "mem"),
            P("mem"),
            P("mem", ("head", "width")),
            P("mem", ("head", "width")),
            P(("head", "width"), "mem"),
        ),
        out_specs=P("groups", "mem"),
        check_vma=False,
    )
```

time: 319 us -> 108 us (0.34)
  waiting for transfers between devices: 130 us -> 0 us
  Pallas kernels: 0 us -> 96.9 us
  blocking collectives: 87.9 us -> 0 us
  matrix products: 47.6 us -> 0 us
  between operations: 14.6 us -> 0.04 us
  local copies, waits for them, and re-layouts: 21.2 us -> 7.08 us
  other arithmetic: 15.7 us -> 3.87 us
    pallas_call x0 -> x3, Pallas kernels: none -> 96.9 us  [the longest x1 60.4 us: per_device(): pl.pallas_call(functools.partial(tail_kernel, n, hwn, q_here), out_shape=...]
    psum x3 -> x0, waiting for transfers between devices: 93.5 us -> none  [the longest x1 32.1 us: per_device(): lax.psum((query_part, key_part, value_part), 'mem')]
    dot_general x25 -> x0, matrix products: 47.6 us -> none  [the longest x1 9.73 us: per_device(): jnp.dot(normed_mid, gate_weight, preferred_element_type=jnp.float32)]
    psum x3 -> x0, blocking collectives: 45.2 us -> none  [the longest x1 20.1 us: per_device(): lax.psum((query_part, key_part, value_part), 'mem')]
    all_gather x3 -> x0, blocking collectives: 42.7 us -> none  [the longest x2 27.5 us: combined_all(): pieces = jax.tree.map(lambda part: lax.all_gather(part, axis), value)]
    reduce_scatter x2 -> x0, waiting for transfers between devices: 36.2 us -> none  [the longest x1 25.2 us: per_device(): lax.psum_scatter(gate_part, 'mem', scatter_dimension=0, tiled=True)]
    dynamic_slice x19 -> x0, local copies, waits for them, and re-layouts: 15.6 us -> none  [the longest x8 15.5 us: visit_block(): lax.dynamic_slice_in_dim(cache_values, first_slot, block_size, 0)]
    reduce_sum x14 -> x1, other arithmetic: 9.19 us -> 1.55 us  [per_device(): jnp.sum((slot_request[None, :] <= ids[:, None]).astype(jnp.int32), axis=1)]
  transfers between devices with their start and end apart: 6 -> 0, of which waited for: 5 -> 0; matrix products, arithmetic and copies ran while one was open for 4% -> 0% of each run, Pallas kernels for 0% -> 0%
where the time goes in v1:
time: 108 us
  Pallas kernels  96.9 us (90%)
  local copies, waits for them, and re-layouts  7.08 us (7%)
  other arithmetic  3.87 us (4%)
    pallas_call x1, Pallas kernels, per_device(): pl.pallas_call(functools.partial(tail_kernel, n, hwn, q_here), out_shape=...  60.4 us
    pallas_call x1, Pallas kernels, per_device(): pl.pallas_call(functools.partial(qkv_kernel, n, q_here, kv), out_shape=ja...  24.3 us
    pallas_call x1, Pallas kernels, per_device(): pl.pallas_call(functools.partial(attend_kernel, n, kv), out_shape=(jax.Sh...  12.2 us

profile of v1, /device:TPU:0, one launch (start us, length us, event | category | flops | bytes accessed | tf_op | source)
XLA Modules:
  0.0 107.8 jit_solution(3783610637949053624)
XLA Ops:
  0.0 0.7 add_convert_fusion
  0.7 0.1 convert_element_type.29
  0.8 0.1 fusion
  1.0 0.7 pad_maximum_fusion
  1.7 1.3 %broadcast_in_dim.8.gain_ref = f32[1,1280]{1,0:T(1,128)} reshape(f32[1280]{0:T(1024)} %param.17) | data formatting | bytes 10240 | tf_op jit(solution)/shard_map/broadcast_in_dim | solution.py:452
  3.0 24.3 %qkv.1 = bf16[4,8,2560]{2,1,0:T(8,128)(2,1)} custom-call(bf16[32,1280]{1,0:T(8,128)(2,1)} %res_ref.1, f32[1,1280]{1,0:T(1,128)} %broadcast_in_dim.8.gain_ref, f32[1,128]{1,0:T(1,128)} %bitcast.15, f32[1,128]{1,0:T(1,128)} %bitcast.16, f32[32,128]{1,0:T(8,128)} %get-tuple-element.16.cos_ref, f32[32,128]{1,0:T(8,128)} %get-tuple-element.17.sin_ref, ...), custom_call_target="tpu_custom_call" | custom-call | tf_op jit(solution)/shard_map/qkv/pallas_call | solution.py:432
  27.2 0.7 slice_convert_fusion
  28.0 0.6 reshape.58.nk_ref
  28.6 0.6 reshape.59.nv_ref
  29.2 0.9 slice.12
  30.1 0.7 reshape.52.q_ref
  30.9 1.5 %convert_reduce_fusion = (s32[16]{0:T(128)}, s32[16]{0:T(128)}) fusion(s32[8192]{0:T(1024)} %param.25), kind=kLoop, calls=%fused_computation | loop fusion | flops 786400 | bytes 32896 | tf_op jit(solution)/shard_map/reduce_sum | solution.py:430
  32.4 12.2 %attend.1 = (f32[16,32,128]{2,1,0:T(8,128)}, f32[4,8,128]{2,1,0:T(8,128)}) custom-call(s32[16]{0:T(128)} %get-tuple-element.10.starts, s32[16]{0:T(128)} %get-tuple-element.9.ends, bf16[16,32,128]{2,1,0:T(8,128)(2,1)} %reshape.52.q_ref, f32[16,4,128]{2,1,0:T(4,128)} %reshape.58.nk_ref, f32[16,4,128]{2,1,0:T(4,128)} %reshape.59.nv_ref, ...), custom_call_target="tpu_custom_call" | custom-call | tf_op jit(solution)/shard_map/attend/pallas_call | solution.py:463
  44.6 1.3 %broadcast_in_dim.11.gain_ref = f32[1,1280]{1,0:T(1,128)} reshape(f32[1280]{0:T(1024)} %param.28) | data formatting | bytes 10240 | tf_op jit(solution)/shard_map/broadcast_in_dim | solution.py:520
  45.9 60.4 %tail.1 = bf16[4,8,1280]{2,1,0:T(8,128)(2,1)} custom-call(f32[4,128,128]{2,1,0:T(8,128)} %bitcast.14, f32[4,8,128]{2,1,0:T(8,128)} %get-tuple-element.8.st_ref, bf16[4,8,1280]{2,1,0:T(8,128)(2,1)} %bitcast.13, f32[1,1280]{1,0:T(1,128)} %broadcast_in_dim.11.gain_ref, bf16[2048,1280]{1,0:T(8,128)(2,1)} %wo_h.1, bf16[1280,6400]{1,0:T(8,128)(2,1)} %wg_h.1, ...), custom_call_target="tpu_custom_call" | custom-call | tf_op jit(solution)/shard_map/tail/pallas_call | solution.py:484
  106.3 1.5 %copy.18 = bf16[32,1280]{1,0:T(8,128)(2,1)} copy(bf16[32,1280]{1,0:T(8,128)(2,1)} %bitcast.12) | data formatting | bytes 163840
  (1 shorter events, 0.0 us)
